TPU v7x, 512 devices: a whole 4x4x16 slice. The times are simulated.
512 devices in a mesh: prow: 16 (over y_hi, x, core), pcol: 32 (over y_lo, z).
Axes of the slice: x: 4, y: 4 (y_hi: 2, y_lo: 2; y = y_hi * 2 + y_lo), z: 16, core: 2. Of those that a mesh axis runs over, the one named last changes fastest.
Arguments:
- sep_inverse: bfloat16 [2, 16, 256, 1, 32, 256], P(None, 'prow', None, None, 'pcol'), may hold values from -2 to 30, as said below
- panels: bfloat16 [4, 2, 16, 256, 256], P(None, None, 'prow', 'pcol'), may hold values from -0.0625 to 0.0625
- ancestors: int32 [4, 32], replicated, may hold values from 0 to 1, as said below
- window_factor: bfloat16 [6, 256, 256], replicated, may hold values from -0.1875 to 0.1875
- diag_inverse: bfloat16 [4, 256, 256], replicated, may hold values from -1 to 4, as said below
Outputs:
- ys: float32 [4, 2, 16, 256, 256], P(None, None, 'prow', 'pcol')
- window_inverse: float32 [1024, 1024], P('prow', 'pcol')
Inputs may be any that keep to these rules, and one draw needn't show every extreme that they name: sep_inverse read as in the first step is symmetric. `diag_inverse`: each block is symmetric. ancestors[k + 1, t] <= ancestors[k, t]: a supernode's ancestor tiles lie among those of the one before it.
All inputs are finite; a program needn't handle non-finite values.
Results may differ from a plain program's by a relative error of at most 0.00035.
Values may be sent and summed in bfloat16 or wider, within the bound.
A program may use at most 64 MiB of HBM per device.

v0:
```python
import jax
import jax.numpy as jnp
from jax import lax
from jax.sharding import PartitionSpec as P


def broadcast(block, axis, owner):
    block = jnp.where(lax.axis_index(axis) == owner, block, jnp.zeros_like(block))
    return lax.psum(block, axis)


def product(operand_left, operand_right):
    return jnp.dot(
        operand_left,
        operand_right,
        precision=lax.Precision.HIGHEST,
        preferred_element_type=jnp.float32,
    )


def pair_index(earlier, later):
    return later * (later - 1) // 2 + earlier


def window_step(later, window_sums, window_factor, diag_inverse, window_blocks):
    coupled = []
    for earlier in range(later):
        running = window_sums[earlier]
        for partner in range(later):
            running = running + product(
                window_blocks[earlier, partner],
                window_factor[pair_index(partner, later)].astype(jnp.float32),
            )
        upper_block = -running
        window_blocks[earlier, later] = upper_block
        window_blocks[later, earlier] = upper_block.T
        coupled.append(upper_block)
    running = window_sums[later]
    for earlier in range(later):
        running = running + product(
            window_factor[pair_index(earlier, later)].astype(jnp.float32).T, coupled[earlier]
        )
    window_blocks[later, later] = diag_inverse[later].astype(jnp.float32) - running


def assemble_window(window_blocks, supernodes):
    return jnp.block(
        [
            [window_blocks[first, second] for second in range(supernodes)]
            for first in range(supernodes)
        ]
    )


def per_device(sep_inverse, panels, ancestors, window_factor, diag_inverse):
    prow_count = lax.axis_size("prow")
    pcol_count = lax.axis_size("pcol")
    row_index = lax.axis_index("prow")
    column_index = lax.axis_index("pcol")
    tile_rows = sep_inverse.shape[0]
    width = sep_inverse.shape[2]
    owned_count = sep_inverse.shape[3]
    supernodes = panels.shape[0]
    slice_rows = panels.shape[3]
    group_ratio = pcol_count // prow_count
    local_sep = sep_inverse.reshape(tile_rows, width, owned_count, width)
    window_blocks = {}
    columns = []
    for later in range(supernodes):
        tile_flags = lax.dynamic_slice_in_dim(
            ancestors[later].reshape(tile_rows, prow_count), row_index, 1, 1
        )
        keep_tiles = tile_flags.astype(jnp.bfloat16).reshape(tile_rows, 1, 1)
        own_piece = panels[later, :, 0] * keep_tiles
        full_rows = lax.all_gather(own_piece, "pcol", axis=1, tiled=True)
        grouped = full_rows.reshape(owned_count, group_ratio, width, width)
        picked = lax.dynamic_slice_in_dim(grouped, column_index // prow_count, 1, 1)[:, 0]
        owned_tiles = broadcast(picked, "prow", column_index % prow_count)

        def row_term(first_row, row_count, owned_tiles=owned_tiles):
            return jnp.einsum(
                "rbcd,cde->bre", local_sep, owned_tiles, preferred_element_type=jnp.float32
            )

        summed = lax.psum_scatter(
            row_term(jnp.int32(0), slice_rows * lax.axis_size("pcol")),
            "pcol",
            scatter_dimension=0,
            tiled=True,
        )
        row_total = jnp.transpose(summed, (1, 0, 2)).reshape(tile_rows * slice_rows, width)
        row_keep = jnp.repeat(
            tile_flags[:, 0].astype(jnp.float32),
            slice_rows,
            total_repeat_length=tile_rows * slice_rows,
        )
        carried = -row_total
        for earlier in range(later):
            carried = carried - product(
                columns[earlier], window_factor[pair_index(earlier, later)].astype(jnp.float32)
            )
        current = carried * row_keep[:, None]
        factor_rows = own_piece.reshape(tile_rows * slice_rows, width).astype(jnp.float32)
        window_parts = [product(columns[earlier].T, factor_rows) for earlier in range(later)]
        window_parts.append(product(factor_rows.T, current))
        window_sums = lax.psum(jnp.stack(window_parts), ("prow", "pcol"))
        window_step(later, window_sums, window_factor, diag_inverse, window_blocks)
        columns.append(current)
    ys = jnp.stack(columns).reshape(supernodes, tile_rows, 1, slice_rows, width)
    whole_window = assemble_window(window_blocks, supernodes)
    rows_each = supernodes * width // prow_count
    cols_each = supernodes * width // pcol_count
    local_window = lax.dynamic_slice(
        whole_window, (row_index * rows_each, column_index * cols_each), (rows_each, cols_each)
    )
    return (ys, local_window)


def solution(mesh):
    placed = (
        P(None, "prow", None, None, "pcol", None),
        P(None, None, "prow", "pcol", None),
        P(),
        P(),
        P(),
    )
    return jax.shard_map(
        per_device,
        mesh=mesh,
        in_specs=placed,
        out_specs=(P(None, None, "prow", "pcol", None), P("prow", "pcol")),
        check_vma=False,
    )
```

profile of v0, /device:TPU:4, one launch (start us, length us, event | category | flops | bytes accessed | tf_op | source)
XLA Modules:
  0.0 1206.1 jit_solution(4849116906709062268)
XLA Ops:
  7.3 0.8 slice_reduce_fusion.1
  8.9 0.8 bitcast_multiply_fusion.6
  9.8 70.2 %all_gather.12 = bf16[2,256,256]{2,0,1:T(2,128)(2,1)S(1)} all-gather(bf16[2,8,256]{2,0,1:T(2,128)(2,1)S(1)} %copy.58), channel_id=1, replica_groups=mesh['prow'=16,'pcol'=32] {'pcol'}, dimensions={1}, use_global_device_ids=true | all-gather | bytes 270336 | tf_op jit(solution)/shard_map/all_gather | solution.py:75
  80.4 59.8 %all_gather.13 = bf16[2,256,256]{2,0,1:T(2,128)(2,1)S(1)} all-gather(bf16[2,8,256]{2,0,1:T(2,128)(2,1)S(1)} %copy.63), channel_id=1, replica_groups=mesh['prow'=16,'pcol'=32] {'pcol'}, dimensions={1}, use_global_device_ids=true | all-gather | bytes 270336 | tf_op jit(solution)/shard_map/all_gather | solution.py:75
  140.7 0.7 select_bitcast_fusion.3
  141.3 0.6 select_bitcast_fusion.2
  142.0 61.7 %all_gather.15 = bf16[2,256,256]{2,0,1:T(2,128)(2,1)S(1)} all-gather(bf16[2,8,256]{2,0,1:T(2,128)(2,1)S(1)} %copy.73), channel_id=1, replica_groups=mesh['prow'=16,'pcol'=32] {'pcol'}, dimensions={1}, use_global_device_ids=true | all-gather | bytes 270336 | tf_op jit(solution)/shard_map/all_gather | solution.py:75
  204.1 0.7 select_bitcast_fusion
  204.8 59.8 %all_gather.14 = bf16[2,256,256]{2,0,1:T(2,128)(2,1)S(1)} all-gather(bf16[2,8,256]{2,0,1:T(2,128)(2,1)S(1)} %copy.68), channel_id=1, replica_groups=mesh['prow'=16,'pcol'=32] {'pcol'}, dimensions={1}, use_global_device_ids=true | all-gather | bytes 270336 | tf_op jit(solution)/shard_map/all_gather | solution.py:75
  265.0 0.7 select_bitcast_fusion.1
  265.8 141.1 %all-reduce.15.cloned.1.call-done = (bf16[256,256]{0,1:T(8,128)(2,1)}, bf16[256,256]{0,1:T(8,128)(2,1)}, bf16[256,256]{0,1:T(8,128)(2,1)}, bf16[256,256]{0,1:T(8,128)(2,1)}) async-done(((bf16[256,256]{0,1:T(8,128)(2,1)}, bf16[256,256]{0,1:T(8,128)(2,1)}, bf16[256,256]{0,1:T(8,128)(2,1)}, bf16[256,256]{0,1:T(8,128)(2,1)}), (bf16[256,256]{0,1:T(8,128)(2,1)}, bf16[256,256]{0,1:T(8,128)(2,1)}, ...) | async-done | bytes 524304 | tf_op jit(solution)/shard_map/psum | solution.py:9
  406.9 1.2 convolution_bitcast_fusion
  408.1 1.0 copy.75
  409.3 1.0 copy.60
  410.6 1.0 copy.65
  411.9 1.0 copy.70
  414.1 0.6 fusion.134
  414.7 0.6 fusion.135
  415.3 0.7 fusion.136
  415.9 0.6 fusion.137
  416.5 5.0 broadcast_select_fusion
  421.6 1.3 dynamic-slice.31
  423.5 262.1 %all-reduce.13.cloned.1.call-done = (f32[256,2,256]{2,1,0:T(2,128)}, f32[256,2,256]{2,1,0:T(2,128)}, f32[256,2,256]{2,1,0:T(2,128)}, f32[256,2,256]{2,1,0:T(2,128)}) async-done(((f32[256,2,256]{2,1,0:T(2,128)}, f32[256,2,256]{2,1,0:T(2,128)}, f32[256,2,256]{2,1,0:T(2,128)}, f32[256,2,256]{2,1,0:T(2,128)}), (f32[256,2,256]{2,1,0:T(2,128)}, f32[256,2,256]{2,1,0:T(2,128)}, f32[256,2,256]{2,1,0:T(2,128)}, ...) | async-done | bytes 2097168
  685.7 0.7 constant_dynamic-slice_fusion.11
  686.4 0.4 convolution_bitcast_fusion.13
  686.8 0.4 convolution_bitcast_fusion.16
  687.2 0.4 convolution_bitcast_fusion.18
  687.6 1.1 convolution_bitcast_fusion.19
  688.7 0.7 constant_dynamic-slice_fusion.10
  689.4 0.7 constant_dynamic-slice_fusion.9
  690.5 0.3 convolution_bitcast_fusion.15
  691.0 0.4 convolution_bitcast_fusion.14
  691.5 0.3 convolution_bitcast_fusion.11
  691.8 0.3 convolution_bitcast_fusion.12
  692.1 0.7 constant_dynamic-slice_fusion.8
  693.2 0.4 convolution_bitcast_fusion.17
  693.8 0.4 convolution_bitcast_fusion.10
  694.2 0.8 pad_maximum_fusion.2
  695.0 0.9 pad_maximum_fusion.1
  696.0 1.1 pad_maximum_fusion
  697.2 0.6 pad_maximum_fusion.3
  697.8 481.1 %all-reduce.11.cloned.1.call-done = (f32[1,256,256]{2,1,0:T(8,128)}, f32[4,256,256]{2,1,0:T(8,128)}, f32[2,256,256]{2,1,0:T(8,128)}, f32[3,256,256]{2,1,0:T(8,128)}) async-done(((f32[1,256,256]{2,1,0:T(8,128)}, f32[4,256,256]{2,1,0:T(8,128)}, f32[2,256,256]{2,1,0:T(8,128)}, f32[3,256,256]{2,1,0:T(8,128)}), (f32[1,256,256]{2,1,0:T(8,128)}, f32[4,256,256]{2,1,0:T(8,128)}, f32[2,256,256]{2,1,0:T(8,128)}, ...) | async-done | bytes 2621456 | tf_op jit(solution)/shard_map/psum | solution.py:106
  1178.9 1.0 subtract_bitcast_fusion
  1179.9 1.3 fusion.14
  1181.2 0.3 fusion.11
  1181.6 0.4 convolution_add_fusion.5
  1182.2 0.4 copy-done.5
  1182.7 0.4 convolution_add_fusion.7
  1183.6 1.0 fusion.7
  1184.7 0.4 convolution_add_fusion.2
  1185.1 0.8 copy.82
  1186.7 0.9 copy.86
  1187.6 0.9 copy.91
  1189.0 0.4 copy-done.4
  1189.4 1.2 fusion.6
  1190.6 0.8 copy.85
  1191.4 2.0 fusion.3
  1193.4 0.8 copy.90
  1194.3 0.4 convolution_add_fusion.1
  1194.7 0.6 copy-done.3
  1195.2 0.3 fusion.2
  1195.8 1.9 fusion.1
  1197.9 1.1 maximum_maximum_fusion
  1198.9 0.7 copy.93
  (76 shorter events, 8.4 us)
Async XLA Ops:
  7.2 399.7 %copy-start = (bf16[2,1,256,1,1,256]{5,2,4,3,1,0:T(8,128)(2,1)S(1)}, bf16[2,1,256,1,1,256]{5,2,4,3,1,0:T(8,128)(2,1)}, u32[]{:S(2)}) copy-start(bf16[2,1,256,1,1,256]{5,2,4,3,1,0:T(8,128)(2,1)} %param.15) | copy-start | bytes 786436
  7.2 399.7 %all-reduce.15.cloned.1.call-start = ((), (), s32[]{:S(2)}) async-start(), calls=%async_computation.2 | async-start | bytes 1048576 | tf_op jit(solution)/shard_map/psum | solution.py:9
  265.7 420.0 %all-reduce.13.cloned.1.call-start = ((), (), s32[]{:S(2)}) async-start(), calls=%async_computation.1 | async-start | bytes 4194304
  406.9 2.2 copy-start.11
  409.1 1.3 copy-start.10
  410.3 1.3 copy-start.9
  412.9 3.6 copy-start.12
  412.9 273.5 %copy-start.8 = (bf16[4,2,1,8,256]{4,3,2,1,0:T(8,128)(2,1)S(1)}, bf16[4,2,1,8,256]{4,3,2,1,0:T(8,128)(2,1)}, u32[]{:S(2)}) copy-start(bf16[4,2,1,8,256]{4,3,2,1,0:T(8,128)(2,1)} %param.16) | copy-start | bytes 98308
  412.9 277.2 %copy-start.1 = (bf16[6,256,256]{2,1,0:T(8,128)(2,1)S(1)}, bf16[6,256,256]{2,1,0:T(8,128)(2,1)}, u32[]{:S(2)}) copy-start(bf16[6,256,256]{2,1,0:T(8,128)(2,1)} %param.18) | copy-start | bytes 2359300
  412.9 765.9 %all-reduce.11.cloned.1.call-start = ((), (), s32[]{:S(2)}) async-start(), calls=%async_computation | async-start | bytes 5242880 | tf_op jit(solution)/shard_map/psum | solution.py:106
  697.1 481.8 %copy-start.7 = (bf16[4,256,256]{2,1,0:T(8,128)(2,1)S(1)}, bf16[4,256,256]{2,1,0:T(8,128)(2,1)}, u32[]{:S(2)}) copy-start(bf16[4,256,256]{2,1,0:T(8,128)(2,1)} %param.19) | copy-start | bytes 1572868
  1178.9 2.4 copy-start.6
  1179.9 1.7 copy-start.2
  1181.6 1.1 copy-start.5
  1188.4 0.9 copy-start.4
  1194.3 0.9 copy-start.3
Sparse Core Ops, SparseCore 0:
  265.8 140.9 all-reduce.14
  413.1 272.5 all-reduce.12
  697.2 481.5 all-reduce.10
where the time goes:
time: 1210 us
  waiting for transfers between devices  884 us (73%)
  blocking collectives  252 us (21%)
  local copies, waits for them, and re-layouts  20.5 us (2%)
  matrix products  19.6 us (2%)
  other arithmetic  15 us (1%)
  between operations  14.9 us (1%)
    psum x1, waiting for transfers between devices, per_device(): window_sums = lax.psum(jnp.stack(window_parts), ('prow', 'pcol'))  481 us
    unnamed x4, waiting for transfers between devices  262 us
    all_gather x4, blocking collectives, per_device(): full_rows = lax.all_gather(own_piece, 'pcol', axis=1, tiled=True)  252 us
    psum x1, waiting for transfers between devices, broadcast(): return lax.psum(block, axis)  141 us
  transfers between devices with their start and end apart: 3, of which 3 were waited for; matrix products, arithmetic and copies ran while one was open for 1% of the time, Pallas kernels for 0%

commit v1 on v0

--- a/solution.py
+++ b/solution.py
@@ -103,7 +103,9 @@
         factor_rows = own_piece.reshape(tile_rows * slice_rows, width).astype(jnp.float32)
         window_parts = [product(columns[earlier].T, factor_rows) for earlier in range(later)]
         window_parts.append(product(factor_rows.T, current))
-        window_sums = lax.psum(jnp.stack(window_parts), ("prow", "pcol"))
+        window_sums = jnp.stack(window_parts)
+        for jj in ("prow", "pcol"):
+            window_sums = lax.psum(window_sums, axis_name=jj)
         window_step(later, window_sums, window_factor, diag_inverse, window_blocks)
         columns.append(current)
     ys = jnp.stack(columns).reshape(supernodes, tile_rows, 1, slice_rows, width)

time: 1210 us -> 1150 us (0.950)
  waiting for transfers between devices: 884 us -> 828 us
    psum x1 -> x2, waiting for transfers between devices: 481 us -> 424 us  [per_device(): window_sums = lax.psum(window_sums, axis_name=jj)]
    unnamed x4 -> x5, waiting for transfers between devices: 262 us -> 262 us
  transfers between devices with their start and end apart: 3 -> 4, of which waited for: 3 -> 4; matrix products, arithmetic and copies ran while one was open for 1% -> 1% of each run, Pallas kernels for 0% -> 0%
where the time goes in v1:
time: 1150 us
  waiting for transfers between devices  828 us (72%)
  blocking collectives  252 us (22%)
  local copies, waits for them, and re-layouts  20.5 us (2%)
  matrix products  19.6 us (2%)
  other arithmetic  15 us (1%)
  between operations  14.9 us (1%)
    psum x2, waiting for transfers between devices, per_device(): window_sums = lax.psum(window_sums, axis_name=jj)  424 us
    unnamed x5, waiting for transfers between devices  262 us
    all_gather x4, blocking collectives, per_device(): full_rows = lax.all_gather(own_piece, 'pcol', axis=1, tiled=True)  252 us
    psum x1, waiting for transfers between devices, broadcast(): return lax.psum(block, axis)  141 us
  transfers between devices with their start and end apart: 4, of which 4 were waited for; matrix products, arithmetic and copies ran while one was open for 1% of the time, Pallas kernels for 0%

profile of v1, /device:TPU:4, one launch (start us, length us, event | category | flops | bytes accessed | tf_op | source)
XLA Modules:
  0.0 1149.5 jit_solution(7416847083691873178)
XLA Ops:
  7.3 0.8 slice_reduce_fusion.1
  8.9 0.8 bitcast_multiply_fusion.6
  9.8 70.2 %all_gather.12 = bf16[2,256,256]{2,0,1:T(2,128)(2,1)S(1)} all-gather(bf16[2,8,256]{2,0,1:T(2,128)(2,1)S(1)} %copy.58), channel_id=1, replica_groups=mesh['prow'=16,'pcol'=32] {'pcol'}, dimensions={1}, use_global_device_ids=true | all-gather | bytes 270336 | tf_op jit(solution)/shard_map/all_gather | solution.py:75
  80.4 59.8 %all_gather.13 = bf16[2,256,256]{2,0,1:T(2,128)(2,1)S(1)} all-gather(bf16[2,8,256]{2,0,1:T(2,128)(2,1)S(1)} %copy.63), channel_id=1, replica_groups=mesh['prow'=16,'pcol'=32] {'pcol'}, dimensions={1}, use_global_device_ids=true | all-gather | bytes 270336 | tf_op jit(solution)/shard_map/all_gather | solution.py:75
  140.7 0.7 select_bitcast_fusion.3
  141.3 0.6 select_bitcast_fusion.2
  142.0 61.7 %all_gather.15 = bf16[2,256,256]{2,0,1:T(2,128)(2,1)S(1)} all-gather(bf16[2,8,256]{2,0,1:T(2,128)(2,1)S(1)} %copy.73), channel_id=1, replica_groups=mesh['prow'=16,'pcol'=32] {'pcol'}, dimensions={1}, use_global_device_ids=true | all-gather | bytes 270336 | tf_op jit(solution)/shard_map/all_gather | solution.py:75
  204.1 0.7 select_bitcast_fusion
  204.8 59.8 %all_gather.14 = bf16[2,256,256]{2,0,1:T(2,128)(2,1)S(1)} all-gather(bf16[2,8,256]{2,0,1:T(2,128)(2,1)S(1)} %copy.68), channel_id=1, replica_groups=mesh['prow'=16,'pcol'=32] {'pcol'}, dimensions={1}, use_global_device_ids=true | all-gather | bytes 270336 | tf_op jit(solution)/shard_map/all_gather | solution.py:75
  265.0 0.7 select_bitcast_fusion.1
  265.8 141.1 %all-reduce.19.cloned.1.call-done = (bf16[256,256]{0,1:T(8,128)(2,1)}, bf16[256,256]{0,1:T(8,128)(2,1)}, bf16[256,256]{0,1:T(8,128)(2,1)}, bf16[256,256]{0,1:T(8,128)(2,1)}) async-done(((bf16[256,256]{0,1:T(8,128)(2,1)}, bf16[256,256]{0,1:T(8,128)(2,1)}, bf16[256,256]{0,1:T(8,128)(2,1)}, bf16[256,256]{0,1:T(8,128)(2,1)}), (bf16[256,256]{0,1:T(8,128)(2,1)}, bf16[256,256]{0,1:T(8,128)(2,1)}, ...) | async-done | bytes 524304 | tf_op jit(solution)/shard_map/psum | solution.py:9
  406.9 1.2 convolution_bitcast_fusion
  408.1 1.0 copy.75
  409.3 1.0 copy.60
  410.6 1.0 copy.65
  411.9 1.0 copy.70
  413.9 0.6 fusion.134
  414.5 0.6 fusion.135
  415.1 0.7 fusion.136
  415.8 0.6 fusion.137
  416.3 5.0 broadcast_select_fusion
  421.4 1.3 dynamic-slice.31
  423.4 262.3 %all-reduce.15.cloned.1.call-done = (f32[256,2,256]{2,1,0:T(2,128)}, f32[256,2,256]{2,1,0:T(2,128)}, f32[256,2,256]{2,1,0:T(2,128)}, f32[256,2,256]{2,1,0:T(2,128)}) async-done(((f32[256,2,256]{2,1,0:T(2,128)}, f32[256,2,256]{2,1,0:T(2,128)}, f32[256,2,256]{2,1,0:T(2,128)}, f32[256,2,256]{2,1,0:T(2,128)}), (f32[256,2,256]{2,1,0:T(2,128)}, f32[256,2,256]{2,1,0:T(2,128)}, f32[256,2,256]{2,1,0:T(2,128)}, ...) | async-done | bytes 2097168
  685.6 0.7 constant_dynamic-slice_fusion.11
  686.3 0.4 convolution_bitcast_fusion.13
  686.7 0.4 convolution_bitcast_fusion.16
  687.1 0.4 convolution_bitcast_fusion.18
  687.5 1.1 convolution_bitcast_fusion.19
  688.6 0.7 constant_dynamic-slice_fusion.10
  689.3 0.7 constant_dynamic-slice_fusion.9
  690.5 0.3 convolution_bitcast_fusion.15
  691.0 0.4 convolution_bitcast_fusion.14
  691.4 0.3 convolution_bitcast_fusion.11
  691.7 0.3 convolution_bitcast_fusion.12
  692.1 0.7 constant_dynamic-slice_fusion.8
  693.2 0.4 convolution_bitcast_fusion.17
  693.8 0.4 convolution_bitcast_fusion.10
  694.2 0.8 pad_maximum_fusion.2
  695.0 0.9 pad_maximum_fusion.1
  695.9 1.1 pad_maximum_fusion
  697.2 147.2 %all-reduce.17.cloned.1.call-done = (f32[1,256,256]{2,1,0:T(8,128)}, f32[4,256,256]{2,1,0:T(8,128)}, f32[2,256,256]{2,1,0:T(8,128)}, f32[3,256,256]{2,1,0:T(8,128)}) async-done(((f32[1,256,256]{2,1,0:T(8,128)}, f32[4,256,256]{2,1,0:T(8,128)}, f32[2,256,256]{2,1,0:T(8,128)}, f32[3,256,256]{2,1,0:T(8,128)}), (f32[1,256,256]{2,1,0:T(8,128)}, f32[4,256,256]{2,1,0:T(8,128)}, f32[2,256,256]{2,1,0:T(8,128)}, ...) | async-done | bytes 2621456 | tf_op jit(solution)/shard_map/psum | solution.py:108
  844.5 0.6 pad_maximum_fusion.3
  845.1 277.1 %all-reduce.13.cloned.1.call-done = (f32[1,256,256]{2,1,0:T(8,128)}, f32[4,256,256]{2,1,0:T(8,128)}, f32[2,256,256]{2,1,0:T(8,128)}, f32[3,256,256]{2,1,0:T(8,128)}) async-done(((f32[1,256,256]{2,1,0:T(8,128)}, f32[4,256,256]{2,1,0:T(8,128)}, f32[2,256,256]{2,1,0:T(8,128)}, f32[3,256,256]{2,1,0:T(8,128)}), (f32[1,256,256]{2,1,0:T(8,128)}, f32[4,256,256]{2,1,0:T(8,128)}, f32[2,256,256]{2,1,0:T(8,128)}, ...) | async-done | bytes 2621456 | tf_op jit(solution)/shard_map/psum | solution.py:108
  1122.3 1.0 subtract_bitcast_fusion
  1123.3 1.3 fusion.14
  1124.6 0.3 fusion.11
  1125.0 0.4 convolution_add_fusion.5
  1125.6 0.4 copy-done.5
  1126.1 0.4 convolution_add_fusion.7
  1127.0 1.0 fusion.7
  1128.1 0.4 convolution_add_fusion.2
  1128.4 0.8 copy.82
  1130.1 0.9 copy.86
  1131.0 0.9 copy.91
  1132.4 0.4 copy-done.4
  1132.8 1.2 fusion.6
  1134.0 0.8 copy.85
  1134.8 2.0 fusion.3
  1136.8 0.8 copy.90
  1137.7 0.4 convolution_add_fusion.1
  1138.0 0.6 copy-done.3
  1139.2 1.9 fusion.1
  1141.3 1.1 maximum_maximum_fusion
  1142.3 0.7 copy.93
  (79 shorter events, 8.7 us)
Async XLA Ops:
  7.2 399.7 %copy-start = (bf16[2,1,256,1,1,256]{5,2,4,3,1,0:T(8,128)(2,1)S(1)}, bf16[2,1,256,1,1,256]{5,2,4,3,1,0:T(8,128)(2,1)}, u32[]{:S(2)}) copy-start(bf16[2,1,256,1,1,256]{5,2,4,3,1,0:T(8,128)(2,1)} %param.15) | copy-start | bytes 786436
  7.2 399.7 %all-reduce.19.cloned.1.call-start = ((), (), s32[]{:S(2)}) async-start(), calls=%async_computation.3 | async-start | bytes 1048576 | tf_op jit(solution)/shard_map/psum | solution.py:9
  265.7 419.9 %all-reduce.15.cloned.1.call-start = ((), (), s32[]{:S(2)}) async-start(), calls=%async_computation.1 | async-start | bytes 4194304
  406.9 2.2 copy-start.11
  409.1 1.3 copy-start.10
  410.3 1.3 copy-start.9
  412.9 3.4 copy-start.12
  412.9 273.4 %copy-start.8 = (bf16[4,2,1,8,256]{4,3,2,1,0:T(8,128)(2,1)S(1)}, bf16[4,2,1,8,256]{4,3,2,1,0:T(8,128)(2,1)}, u32[]{:S(2)}) copy-start(bf16[4,2,1,8,256]{4,3,2,1,0:T(8,128)(2,1)} %param.16) | copy-start | bytes 98308
  412.9 277.1 %copy-start.1 = (bf16[6,256,256]{2,1,0:T(8,128)(2,1)S(1)}, bf16[6,256,256]{2,1,0:T(8,128)(2,1)}, u32[]{:S(2)}) copy-start(bf16[6,256,256]{2,1,0:T(8,128)(2,1)} %param.18) | copy-start | bytes 2359300
  412.9 431.5 %all-reduce.17.cloned.1.call-start = ((), (), s32[]{:S(2)}) async-start(), calls=%async_computation.2 | async-start | bytes 5242880 | tf_op jit(solution)/shard_map/psum | solution.py:108
  697.0 425.2 %all-reduce.13.cloned.1.call-start = ((), (), s32[]{:S(2)}) async-start(), calls=%async_computation | async-start | bytes 5242880 | tf_op jit(solution)/shard_map/psum | solution.py:108
  844.4 277.8 %copy-start.7 = (bf16[4,256,256]{2,1,0:T(8,128)(2,1)S(1)}, bf16[4,256,256]{2,1,0:T(8,128)(2,1)}, u32[]{:S(2)}) copy-start(bf16[4,256,256]{2,1,0:T(8,128)(2,1)} %param.19) | copy-start | bytes 1572868
  1122.2 2.4 copy-start.6
  1123.3 1.7 copy-start.2
  1125.0 1.1 copy-start.5
  1131.8 0.9 copy-start.4
  1137.7 0.9 copy-start.3
Sparse Core Ops, SparseCore 0:
  265.8 140.9 all-reduce.18
  413.1 272.5 all-reduce.14
  697.1 147.2 all-reduce.16
  847.4 274.7 all-reduce.12
